TPU v7x, 512 devices: a whole 4x4x16 slice. The times are simulated.
512 devices in a mesh: row: 128 (over y, z, core), col: 4 (over x).
Axes of the slice: x: 4, y: 4, z: 16, core: 2. Of those that a mesh axis runs over, the one named last changes fastest.
Arguments:
- residual: float32 [65536, 128], P('row'), may hold values from -6 to 6
- solution: float32 [65536, 128], P('row'), may hold values from -6 to 6
- near_field_blocks: float32 [256, 4, 256, 256], P('row', 'col'), may hold values from -0.09375 to 0.09375
- near_cols: int32 [256, 4], P('row', 'col'), may hold values from 0 to 255, as said below
- couplings: float32 [256, 64, 16, 16], P('row', 'col'), may hold values from -0.1875 to 0.1875
- far_cols: int32 [256, 64], P('row', 'col'), may hold values from 0 to 255, as said below
- far_count: int32 [256], P('row'), may hold values from 16 to 64, as said below
- col_basis: float32 [256, 16, 256], P('row'), may hold values from -0.375 to 0.375
- row_basis: float32 [256, 16, 256], P('row'), may hold values from -0.75 to 0.75
Outputs:
- solution_next: float32 [65536, 128], P('row')
- hessenberg: float32 [5, 4, 128], replicated
Inputs may be any that keep to these rules, and one draw needn't show every extreme that they name: near_cols[i, 0] = i; the other entries of row cluster i are i + t for distinct nonzero t with |t| <= 2, clipped to 0 .. 255. far_cols[i, p] differs from i by more than 2, counted around the ends of the cluster range. Slots p >= far_count[i] of row cluster i are unused; some row cluster uses all 64 slots.
All inputs are finite; a program needn't handle non-finite values.
Results may differ from a plain program's by a relative error of at most 0.0001.
Values sent between devices are 32-bit elements; how exact they have to be, the bound alone decides.
A program may use at most 64 MiB of HBM per device.

v0:
```python
import jax
import jax.numpy as jnp
from jax import lax
from jax.sharding import PartitionSpec as P

LEAF_UNKNOWNS = 256
CL_DEV = 2
REACH = 2
SB = 4
HIGH = lax.Precision.HIGHEST
SHIFT = 1.0


def with_halo(value, sides, width):
    for axis, dim in sides:
        peers, length = (lax.axis_size(axis), value.shape[dim])
        up = [(i, (i + 1) % peers) for i in range(peers - 1)]
        down = [(j, i) for i, j in up]
        last = lax.slice_in_dim(value, length - width, length, axis=dim)
        first = lax.slice_in_dim(value, 0, width, axis=dim)
        before = lax.ppermute(last, axis, up)
        after = lax.ppermute(first, axis, down)
        value = jnp.concatenate([before, value, after], axis=dim)
    return value


def cholesky_upper(entries, order_n):
    zero_entry = jnp.zeros_like(entries[0][0])
    upper_r = []
    for row_idx in range(order_n):
        upper_r.append([zero_entry] * order_n)
    for row_idx in range(order_n):
        running = entries[row_idx][row_idx]
        for earlier in range(row_idx):
            running = running - upper_r[earlier][row_idx] * upper_r[earlier][row_idx]
        pivot_val = jnp.sqrt(running)
        upper_r[row_idx][row_idx] = pivot_val
        for col_idx in range(row_idx + 1, order_n):
            entry_val = entries[row_idx][col_idx]
            for earlier in range(row_idx):
                entry_val = entry_val - upper_r[earlier][row_idx] * upper_r[earlier][col_idx]
            upper_r[row_idx][col_idx] = entry_val / pivot_val
    return upper_r


def small_update(gram_sum, scale_factor, depth_n):
    order_n = depth_n + 1
    entries = [
        [gram_sum[row_idx, col_idx] for col_idx in range(order_n)] for row_idx in range(order_n)
    ]
    upper_r = cholesky_upper(entries, order_n)
    shifted = [
        [
            SHIFT * upper_r[row_idx][col_idx] + upper_r[row_idx][col_idx + 1]
            for col_idx in range(depth_n)
        ]
        for row_idx in range(order_n)
    ]
    hessen = []
    for row_idx in range(order_n):
        row_vals = []
        for col_idx in range(depth_n):
            entry_val = shifted[row_idx][col_idx]
            for earlier in range(col_idx):
                entry_val = entry_val - row_vals[earlier] * upper_r[earlier][col_idx]
            row_vals.append(entry_val / upper_r[col_idx][col_idx])
        hessen.append(row_vals)
    normal = []
    for row_idx in range(depth_n):
        row_vals = []
        for col_idx in range(depth_n):
            entry_val = hessen[0][row_idx] * hessen[0][col_idx]
            for inner in range(1, order_n):
                entry_val = entry_val + hessen[inner][row_idx] * hessen[inner][col_idx]
            row_vals.append(entry_val)
        normal.append(row_vals)
    target = [scale_factor * upper_r[0][0] * hessen[0][col_idx] for col_idx in range(depth_n)]
    factor = cholesky_upper(normal, depth_n)
    forward = []
    for row_idx in range(depth_n):
        entry_val = target[row_idx]
        for earlier in range(row_idx):
            entry_val = entry_val - factor[earlier][row_idx] * forward[earlier]
        forward.append(entry_val / factor[row_idx][row_idx])
    solved = [None] * depth_n
    for row_idx in range(depth_n - 1, -1, -1):
        entry_val = forward[row_idx]
        for later in range(row_idx + 1, depth_n):
            entry_val = entry_val - factor[row_idx][later] * solved[later]
        solved[row_idx] = entry_val / factor[row_idx][row_idx]
    weights = [None] * depth_n
    for row_idx in range(depth_n - 1, -1, -1):
        entry_val = solved[row_idx]
        for later in range(row_idx + 1, depth_n):
            entry_val = entry_val - upper_r[row_idx][later] * weights[later]
        weights[row_idx] = entry_val / upper_r[row_idx][row_idx]
    hess_array = jnp.stack([jnp.stack(hessen[row_idx], 0) for row_idx in range(order_n)], 0)
    return (hess_array, weights)


def local(
    residual,
    solution,
    near_field_blocks,
    near_cols,
    couplings,
    far_cols,
    far_count,
    col_basis,
    row_basis,
):
    first_cluster = lax.axis_index("row") * CL_DEV
    blocks, couple = (near_field_blocks, couplings)
    near_idx, far_idx = (near_cols, far_cols)
    positions = lax.axis_index("col") * couplings.shape[1] + jnp.arange(
        couplings.shape[1], dtype=jnp.int32
    )
    live_mask = (positions[None, :] < far_count[:, None]).astype(jnp.float32)
    weighted = couple * live_mask[:, :, None, None]
    local_near = near_idx - (first_cluster - REACH)
    scale_factor = jnp.ones((residual.shape[1],), jnp.float32)
    current = residual
    basis_list = [current]
    for step_k in range(SB):
        width_r = current.shape[1]
        extended = with_halo(current, (("row", 0),), REACH * LEAF_UNKNOWNS)
        panels = extended.reshape(CL_DEV + 2 * REACH, LEAF_UNKNOWNS, width_r)
        picked = jnp.take(panels, local_near, axis=0)
        near_part = jnp.einsum("csab,csbr->car", blocks, picked, precision=HIGH)
        own_panels = current.reshape(CL_DEV, LEAF_UNKNOWNS, width_r)
        coeffs = jnp.einsum("ckb,cbr->ckr", col_basis, own_panels, precision=HIGH)
        table = lax.all_gather(coeffs, "row", axis=0, tiled=True)
        fetched = jnp.take(table, far_idx, axis=0)
        summed = jnp.einsum("cfkl,cflr->ckr", weighted, fetched, precision=HIGH)
        far_part = jnp.einsum("ckb,ckr->cbr", row_basis, summed, precision=HIGH)
        partial_value = (near_part + far_part).reshape(CL_DEV * LEAF_UNKNOWNS, width_r)
        current = lax.psum(partial_value, "col")
        basis_list.append(current)
    stacked = jnp.stack(basis_list, 0)
    local_gram = jnp.einsum("anr,bnr->abr", stacked, stacked, precision=HIGH)
    gram_sum = lax.psum(local_gram, "row")
    hessenberg, weights = small_update(gram_sum, scale_factor, SB)
    new_sol = solution
    for step_k in range(SB):
        new_sol = new_sol + weights[step_k][None, :] * basis_list[step_k]
    return (new_sol, hessenberg)


def solution(mesh):
    placed = (
        P("row", None),
        P("row", None),
        P("row", "col", None, None),
        P("row", "col"),
        P("row", "col", None, None),
        P("row", "col"),
        P("row"),
        P("row", None, None),
        P("row", None, None),
    )
    return jax.shard_map(
        local, mesh=mesh, in_specs=placed, out_specs=(P("row", None), P()), check_vma=False
    )
```

profile of v0, /device:TPU:4, one launch (start us, length us, event | category | flops | bytes accessed | tf_op | source)
XLA Modules:
  0.0 1346.1 jit_solution(8567163214037070050)
XLA Ops:
  7.2 1.9 fusion.85
  9.2 1.8 collective-permute-start
  14.5 1.8 collective-permute-done.1
  17.9 139.1 %all-gather.5.cloned.1.call-done = f32[256,16,128]{2,1,0:T(8,128)} async-done(((f32[2,16,128]{2,1,0:T(8,128)}), f32[256,16,128]{2,1,0:T(8,128)}) %all-gather.5.cloned.1.call-update) | async-done | bytes 2097168 | tf_op jit(solution)/shard_map/all_gather | solution.py:132
  157.0 2.2 gather_fusion.1
  162.2 52.8 %all-reduce.5.cloned.1.call-done = f32[512,128]{0,1:T(8,128)} async-done(((f32[512,128]{0,1:T(8,128)}), f32[512,128]{0,1:T(8,128)}) %all-reduce.5.cloned.1.call-update) | async-done | bytes 262160 | tf_op jit(solution)/shard_map/psum | solution.py:137
  217.1 1.3 collective-permute-start.2
  219.7 4.1 collective-permute-done.3
  225.7 135.3 %all-gather.7.cloned.1.call-done = f32[256,16,128]{2,1,0:T(8,128)} async-done(((f32[2,16,128]{2,1,0:T(8,128)}), f32[256,16,128]{2,1,0:T(8,128)}) %all-gather.7.cloned.1.call-update) | async-done | bytes 2097168 | tf_op jit(solution)/shard_map/all_gather | solution.py:132
  360.9 2.2 gather_fusion.3
  366.2 52.8 %all-reduce.7.cloned.1.call-done = f32[512,128]{0,1:T(8,128)} async-done(((f32[512,128]{0,1:T(8,128)}), f32[512,128]{0,1:T(8,128)}) %all-reduce.7.cloned.1.call-update) | async-done | bytes 262160 | tf_op jit(solution)/shard_map/psum | solution.py:137
  423.6 4.1 collective-permute-done.5
  429.6 135.1 %all-gather.9.cloned.1.call-done = f32[256,16,128]{2,1,0:T(8,128)} async-done(((f32[2,16,128]{2,1,0:T(8,128)}), f32[256,16,128]{2,1,0:T(8,128)}) %all-gather.9.cloned.1.call-update) | async-done | bytes 2097168 | tf_op jit(solution)/shard_map/all_gather | solution.py:132
  564.7 2.2 gather_fusion.5
  569.9 52.8 %all-reduce.9.cloned.1.call-done = f32[512,128]{0,1:T(8,128)} async-done(((f32[512,128]{0,1:T(8,128)}), f32[512,128]{0,1:T(8,128)}) %all-reduce.9.cloned.1.call-update) | async-done | bytes 262160 | tf_op jit(solution)/shard_map/psum | solution.py:137
  626.1 1.5 collective-permute-start.7
  627.6 3.9 collective-permute-done.7
  633.4 135.3 %all-gather.11.cloned.1.call-done = f32[256,16,128]{2,1,0:T(8,128)} async-done(((f32[2,16,128]{2,1,0:T(8,128)}), f32[256,16,128]{2,1,0:T(8,128)}) %all-gather.11.cloned.1.call-update) | async-done | bytes 2097168 | tf_op jit(solution)/shard_map/all_gather | solution.py:132
  768.6 2.2 gather_fusion.7
  779.2 47.4 %all-reduce.11.cloned.1.call-done = f32[1,512,128]{1,0,2:T(1,128)} async-done(((f32[1,512,128]{1,0,2:T(1,128)}), f32[1,512,128]{1,0,2:T(1,128)}) %all-reduce.11.cloned.1.call-update) | async-done | bytes 262160 | tf_op jit(solution)/shard_map/psum | solution.py:137
  826.6 4.6 stack.76
  831.2 3.7 convolution_bitcast_fusion
  834.9 495.3 %psum.39 = f32[5,5,128]{0,1,2:T(8,128)S(1)} all-reduce(f32[5,5,128]{0,1,2:T(8,128)} %convolution_bitcast_fusion), channel_id=1, replica_groups=mesh['row'=128,'col'=4] {'row'}, use_global_device_ids=true, to_apply=%region_4.7 | all-reduce | flops 3200 | bytes 25600 | tf_op jit(solution)/shard_map/psum | solution.py:141
  1330.2 6.9 multiply_reduce_fusion
  (115 shorter events, 41.4 us)
Async XLA Ops:
  7.2 153.2 %copy-start = (f32[2,1,256,256]{3,2,1,0:T(8,128)S(1)}, f32[2,1,256,256]{3,2,1,0:T(8,128)}, u32[]{:S(2)}) copy-start(f32[2,1,256,256]{3,2,1,0:T(8,128)} %param.15) | copy-start | bytes 1572868
  7.2 152.0 %copy-start.1 = (f32[2,16,16,16]{3,2,1,0:T(8,128)S(1)}, f32[2,16,16,16]{3,2,1,0:T(8,128)}, u32[]{:S(2)}) copy-start(f32[2,16,16,16]{3,2,1,0:T(8,128)} %param.17) | copy-start | bytes 98308
  7.2 152.7 %copy-start.9 = (f32[2,16,256]{2,1,0:T(8,128)S(1)}, f32[2,16,256]{2,1,0:T(8,128)}, u32[]{:S(2)}) copy-start(f32[2,16,256]{2,1,0:T(8,128)} %param.21) | copy-start | bytes 98308
  7.2 149.8 %all-gather.5.cloned.1.call-start = ((), (), s32[]{:S(2)}) async-start(), calls=%async_computation | async-start | bytes 2113536 | tf_op jit(solution)/shard_map/all_gather | solution.py:132
  9.2 205.9 %all-reduce.5.cloned.1.call-start = ((), (), s32[]{:S(2)}) async-start(), calls=%async_computation.1 | async-start | bytes 524288 | tf_op jit(solution)/shard_map/psum | solution.py:137
  9.2 5.3 collective-permute-start
  11.0 5.3 collective-permute-start.1
  159.1 57.0 %copy-start.8 = (f32[2,16,256]{2,1,0:T(8,128)S(1)}, f32[2,16,256]{2,1,0:T(8,128)}, u32[]{:S(2)}) copy-start(f32[2,16,256]{2,1,0:T(8,128)} %param.20) | copy-start | bytes 98308
  162.2 198.8 %all-gather.7.cloned.1.call-start = ((), (), s32[]{:S(2)}) async-start(), calls=%async_computation.2 | async-start | bytes 2113536 | tf_op jit(solution)/shard_map/all_gather | solution.py:132
  217.0 201.9 %all-reduce.7.cloned.1.call-start = ((), (), s32[]{:S(2)}) async-start(), calls=%async_computation.3 | async-start | bytes 524288 | tf_op jit(solution)/shard_map/psum | solution.py:137
  217.1 2.7 collective-permute-start.2
  218.4 5.4 collective-permute-start.3
  366.1 198.6 %all-gather.9.cloned.1.call-start = ((), (), s32[]{:S(2)}) async-start(), calls=%async_computation.4 | async-start | bytes 2113536 | tf_op jit(solution)/shard_map/all_gather | solution.py:132
  420.9 201.8 %all-reduce.9.cloned.1.call-start = ((), (), s32[]{:S(2)}) async-start(), calls=%async_computation.5 | async-start | bytes 524288 | tf_op jit(solution)/shard_map/psum | solution.py:137
  421.0 2.7 collective-permute-start.4
  422.3 5.4 collective-permute-start.5
  569.9 198.7 %all-gather.11.cloned.1.call-start = ((), (), s32[]{:S(2)}) async-start(), calls=%async_computation.6 | async-start | bytes 2113536 | tf_op jit(solution)/shard_map/all_gather | solution.py:132
  624.7 201.9 %all-reduce.11.cloned.1.call-start = ((), (), s32[]{:S(2)}) async-start(), calls=%async_computation.7 | async-start | bytes 524288 | tf_op jit(solution)/shard_map/psum | solution.py:137
  624.8 2.8 collective-permute-start.6
  626.1 5.4 collective-permute-start.7
  633.3 140.5 %copy-start.2 = (f32[512,128]{1,0:T(8,128)S(1)}, f32[512,128]{1,0:T(8,128)}, u32[]{:S(2)}) copy-start(f32[512,128]{1,0:T(8,128)} %param.13) | copy-start | bytes 786436
  772.8 5.5 copy-start.5
  834.9 502.6 %copy-start.6 = (f32[512,128]{0,1:T(8,128)S(1)}, f32[512,128]{0,1:T(8,128)}, u32[]{:S(2)}) copy-start(f32[512,128]{0,1:T(8,128)} %copy.65) | copy-start | bytes 786436
  834.9 502.6 %copy-start.7 = (f32[512,128]{0,1:T(8,128)S(1)}, f32[512,128]{0,1:T(8,128)}, u32[]{:S(2)}) copy-start(f32[512,128]{0,1:T(8,128)} %copy.66) | copy-start | bytes 786436
  (4 other events, 14.2 us)
Sparse Core Ops, SparseCore 0:
  11.7 145.1 all-gather.4
  162.3 52.7 all-reduce.4
  218.8 142.1 all-gather.6
  366.2 52.6 all-reduce.6
  422.5 142.1 all-gather.8
  570.0 52.7 all-reduce.8
  626.5 142.1 all-gather.10
  773.9 52.6 all-reduce.10
where the time goes:
time: 1350 us
  waiting for transfers between devices  765 us (57%)
  blocking collectives  495 us (37%)
  local copies, waits for them, and re-layouts  30.2 us (2%)
  matrix products  16.2 us (1%)
  between operations  14.7 us (1%)
  other arithmetic  13.6 us (1%)
    all_gather x4, waiting for transfers between devices, local(): table = lax.all_gather(coeffs, 'row', axis=0, tiled=True)  545 us
    psum x1, blocking collectives, local(): gram_sum = lax.psum(local_gram, 'row')  495 us
    psum x4, waiting for transfers between devices, local(): current = lax.psum(partial_value, 'col')  206 us
  transfers between devices with their start and end apart: 16, of which 12 were waited for; matrix products, arithmetic and copies ran while one was open for 1% of the time, Pallas kernels for 0%

commit v1 on v0

--- a/solution.py
+++ b/solution.py
@@ -129,7 +129,9 @@
         near_part = jnp.einsum("csab,csbr->car", blocks, picked, precision=HIGH)
         own_panels = current.reshape(CL_DEV, LEAF_UNKNOWNS, width_r)
         coeffs = jnp.einsum("ckb,cbr->ckr", col_basis, own_panels, precision=HIGH)
-        table = lax.all_gather(coeffs, "row", axis=0, tiled=True)
+        table = jnp.concatenate(
+            lax.all_to_all(jnp.stack([coeffs] * lax.axis_size("row")), "row", 0, 0), axis=0
+        )
         fetched = jnp.take(table, far_idx, axis=0)
         summed = jnp.einsum("cfkl,cflr->ckr", weighted, fetched, precision=HIGH)
         far_part = jnp.einsum("ckb,ckr->cbr", row_basis, summed, precision=HIGH)

time: 1350 us -> 1240 us (0.919)
  waiting for transfers between devices: 765 us -> 584 us
  starting transfers between devices: 11.3 us -> 84.7 us
    all_gather x4 -> x0, waiting for transfers between devices: 545 us -> none  [local(): table = lax.all_gather(coeffs, 'row', axis=0, tiled=True)]
    all_to_all x0 -> x4, waiting for transfers between devices: none -> 366 us  [local(): lax.all_to_all(jnp.stack([coeffs] * lax.axis_size('row')), 'row', 0, 0)]
    all_to_all x0 -> x4, starting transfers between devices: none -> 73.2 us  [local(): lax.all_to_all(jnp.stack([coeffs] * lax.axis_size('row')), 'row', 0, 0)]
where the time goes in v1:
time: 1240 us
  waiting for transfers between devices  584 us (47%)
  blocking collectives  496 us (40%)
  starting transfers between devices  84.7 us (7%)
  local copies, waits for them, and re-layouts  36.4 us (3%)
  between operations  14.4 us (1%)
  matrix products  13.7 us (1%)
    psum x1, blocking collectives, local(): gram_sum = lax.psum(local_gram, 'row')  496 us
    all_to_all x4, waiting for transfers between devices, local(): lax.all_to_all(jnp.stack([coeffs] * lax.axis_size('row')), 'row', 0, 0)  366 us
    psum x4, waiting for transfers between devices, local(): current = lax.psum(partial_value, 'col')  205 us
    all_to_all x4, starting transfers between devices, local(): lax.all_to_all(jnp.stack([coeffs] * lax.axis_size('row')), 'row', 0, 0)  73.2 us
  transfers between devices with their start and end apart: 16, of which 12 were waited for; matrix products, arithmetic and copies ran while one was open for 1% of the time, Pallas kernels for 0%

profile of v1, /device:TPU:4, one launch (start us, length us, event | category | flops | bytes accessed | tf_op | source)
XLA Modules:
  0.0 1236.4 jit_solution(1824168152202112509)
XLA Ops:
  10.0 20.6 %all-to-all-start = ((f32[128,2,16,128]{3,2,1,0:T(8,128)}), f32[128,2,16,128]{3,2,1,0:T(8,128)}, u32[]{:S(2)}, u32[]{:S(2)}) async-start(f32[128,2,16,128]{3,2,1,0:T(8,128)} %stack.43), calls=%async_computation | async-start | bytes 4194304 | tf_op jit(solution)/shard_map/all_to_all | solution.py:133
  33.9 3.0 collective-permute-done.1
  37.5 91.6 %all-to-all-done = f32[128,2,16,128]{3,2,1,0:T(8,128)} async-done(((f32[128,2,16,128]{3,2,1,0:T(8,128)}), f32[128,2,16,128]{3,2,1,0:T(8,128)}, u32[]{:S(2)}, u32[]{:S(2)}) %all-to-all-start) | async-done | bytes 2097184 | tf_op jit(solution)/shard_map/all_to_all | solution.py:133
  129.1 2.2 gather_fusion.1
  134.3 52.5 %all-reduce.5.cloned.1.call-done = f32[512,128]{0,1:T(8,128)} async-done(((f32[512,128]{0,1:T(8,128)}), f32[512,128]{0,1:T(8,128)}) %all-reduce.5.cloned.1.call-update) | async-done | bytes 262160 | tf_op jit(solution)/shard_map/psum | solution.py:139
  189.7 17.5 %all-to-all-start.1 = ((f32[128,2,16,128]{3,2,1,0:T(8,128)}), f32[128,2,16,128]{3,2,1,0:T(8,128)}, u32[]{:S(2)}, u32[]{:S(2)}) async-start(f32[128,2,16,128]{3,2,1,0:T(8,128)} %stack.45), calls=%async_computation.1 | async-start | bytes 4194304 | tf_op jit(solution)/shard_map/all_to_all | solution.py:133
  210.1 3.2 collective-permute-done.3
  214.2 91.4 %all-to-all-done.1 = f32[128,2,16,128]{3,2,1,0:T(8,128)} async-done(((f32[128,2,16,128]{3,2,1,0:T(8,128)}), f32[128,2,16,128]{3,2,1,0:T(8,128)}, u32[]{:S(2)}, u32[]{:S(2)}) %all-to-all-start.1) | async-done | bytes 2097184 | tf_op jit(solution)/shard_map/all_to_all | solution.py:133
  305.6 2.2 gather_fusion.3
  310.8 52.7 %all-reduce.7.cloned.1.call-done = f32[512,128]{0,1:T(8,128)} async-done(((f32[512,128]{0,1:T(8,128)}), f32[512,128]{0,1:T(8,128)}) %all-reduce.7.cloned.1.call-update) | async-done | bytes 262160 | tf_op jit(solution)/shard_map/psum | solution.py:139
  366.5 17.5 %all-to-all-start.2 = ((f32[128,2,16,128]{3,2,1,0:T(8,128)}), f32[128,2,16,128]{3,2,1,0:T(8,128)}, u32[]{:S(2)}, u32[]{:S(2)}) async-start(f32[128,2,16,128]{3,2,1,0:T(8,128)} %stack.47), calls=%async_computation.2 | async-start | bytes 4194304 | tf_op jit(solution)/shard_map/all_to_all | solution.py:133
  387.0 3.1 collective-permute-done.5
  391.0 91.4 %all-to-all-done.2 = f32[128,2,16,128]{3,2,1,0:T(8,128)} async-done(((f32[128,2,16,128]{3,2,1,0:T(8,128)}), f32[128,2,16,128]{3,2,1,0:T(8,128)}, u32[]{:S(2)}, u32[]{:S(2)}) %all-to-all-start.2) | async-done | bytes 2097184 | tf_op jit(solution)/shard_map/all_to_all | solution.py:133
  482.4 2.2 gather_fusion.5
  487.6 52.7 %all-reduce.9.cloned.1.call-done = f32[512,128]{0,1:T(8,128)} async-done(((f32[512,128]{0,1:T(8,128)}), f32[512,128]{0,1:T(8,128)}) %all-reduce.9.cloned.1.call-update) | async-done | bytes 262160 | tf_op jit(solution)/shard_map/psum | solution.py:139
  543.3 17.5 %all-to-all-start.3 = ((f32[128,2,16,128]{3,2,1,0:T(8,128)}), f32[128,2,16,128]{3,2,1,0:T(8,128)}, u32[]{:S(2)}, u32[]{:S(2)}) async-start(f32[128,2,16,128]{3,2,1,0:T(8,128)} %stack.49), calls=%async_computation.3 | async-start | bytes 4194304 | tf_op jit(solution)/shard_map/all_to_all | solution.py:133
  563.6 3.2 collective-permute-done.7
  567.8 91.4 %all-to-all-done.3 = f32[128,2,16,128]{3,2,1,0:T(8,128)} async-done(((f32[128,2,16,128]{3,2,1,0:T(8,128)}), f32[128,2,16,128]{3,2,1,0:T(8,128)}, u32[]{:S(2)}, u32[]{:S(2)}) %all-to-all-start.3) | async-done | bytes 2097184 | tf_op jit(solution)/shard_map/all_to_all | solution.py:133
  659.2 2.2 gather_fusion.7
  669.8 47.4 %all-reduce.11.cloned.1.call-done = f32[1,512,128]{1,0,2:T(1,128)} async-done(((f32[1,512,128]{1,0,2:T(1,128)}), f32[1,512,128]{1,0,2:T(1,128)}) %all-reduce.11.cloned.1.call-update) | async-done | bytes 262160 | tf_op jit(solution)/shard_map/psum | solution.py:139
  717.1 4.5 stack.51
  721.6 3.7 convolution_bitcast_fusion
  725.3 495.5 %psum.39 = f32[5,5,128]{0,1,2:T(8,128)S(1)} all-reduce(f32[5,5,128]{0,1,2:T(8,128)} %convolution_bitcast_fusion), channel_id=1, replica_groups=mesh['row'=128,'col'=4] {'row'}, use_global_device_ids=true, to_apply=%region_4.7 | all-reduce | flops 3200 | bytes 25600 | tf_op jit(solution)/shard_map/psum | solution.py:143
  1220.9 6.9 multiply_reduce_fusion
  (125 shorter events, 45.8 us)
Async XLA Ops:
  7.2 125.3 %copy-start = (f32[2,1,256,256]{3,2,1,0:T(8,128)S(1)}, f32[2,1,256,256]{3,2,1,0:T(8,128)}, u32[]{:S(2)}) copy-start(f32[2,1,256,256]{3,2,1,0:T(8,128)} %param.15) | copy-start | bytes 1572868
  10.0 119.1 %all-to-all-start = ((f32[128,2,16,128]{3,2,1,0:T(8,128)}), f32[128,2,16,128]{3,2,1,0:T(8,128)}, u32[]{:S(2)}, u32[]{:S(2)}) async-start(f32[128,2,16,128]{3,2,1,0:T(8,128)} %stack.43), calls=%async_computation | async-start | bytes 4194304 | tf_op jit(solution)/shard_map/all_to_all | solution.py:133
  30.7 100.6 %copy-start.1 = (f32[2,16,16,16]{3,2,1,0:T(8,128)S(1)}, f32[2,16,16,16]{3,2,1,0:T(8,128)}, u32[]{:S(2)}) copy-start(f32[2,16,16,16]{3,2,1,0:T(8,128)} %param.17) | copy-start | bytes 98308
  30.7 101.4 %copy-start.11 = (f32[2,16,256]{2,1,0:T(8,128)S(1)}, f32[2,16,256]{2,1,0:T(8,128)}, u32[]{:S(2)}) copy-start(f32[2,16,256]{2,1,0:T(8,128)} %param.21) | copy-start | bytes 98308
  30.7 156.1 %all-reduce.5.cloned.1.call-start = ((), (), s32[]{:S(2)}) async-start(), calls=%async_computation.4 | async-start | bytes 524288 | tf_op jit(solution)/shard_map/psum | solution.py:139
  30.7 3.1 collective-permute-start
  32.3 4.6 collective-permute-start.1
  131.3 56.6 %copy-start.10 = (f32[2,16,256]{2,1,0:T(8,128)S(1)}, f32[2,16,256]{2,1,0:T(8,128)}, u32[]{:S(2)}) copy-start(f32[2,16,256]{2,1,0:T(8,128)} %param.20) | copy-start | bytes 98308
  189.7 116.0 %all-to-all-start.1 = ((f32[128,2,16,128]{3,2,1,0:T(8,128)}), f32[128,2,16,128]{3,2,1,0:T(8,128)}, u32[]{:S(2)}, u32[]{:S(2)}) async-start(f32[128,2,16,128]{3,2,1,0:T(8,128)} %stack.45), calls=%async_computation.1 | async-start | bytes 4194304 | tf_op jit(solution)/shard_map/all_to_all | solution.py:133
  207.2 156.3 %all-reduce.7.cloned.1.call-start = ((), (), s32[]{:S(2)}) async-start(), calls=%async_computation.5 | async-start | bytes 524288 | tf_op jit(solution)/shard_map/psum | solution.py:139
  207.3 2.8 collective-permute-start.2
  208.7 4.6 collective-permute-start.3
  366.5 116.0 %all-to-all-start.2 = ((f32[128,2,16,128]{3,2,1,0:T(8,128)}), f32[128,2,16,128]{3,2,1,0:T(8,128)}, u32[]{:S(2)}, u32[]{:S(2)}) async-start(f32[128,2,16,128]{3,2,1,0:T(8,128)} %stack.47), calls=%async_computation.2 | async-start | bytes 4194304 | tf_op jit(solution)/shard_map/all_to_all | solution.py:133
  384.0 156.3 %all-reduce.9.cloned.1.call-start = ((), (), s32[]{:S(2)}) async-start(), calls=%async_computation.6 | async-start | bytes 524288 | tf_op jit(solution)/shard_map/psum | solution.py:139
  384.1 3.0 collective-permute-start.4
  385.5 4.6 collective-permute-start.5
  543.3 116.0 %all-to-all-start.3 = ((f32[128,2,16,128]{3,2,1,0:T(8,128)}), f32[128,2,16,128]{3,2,1,0:T(8,128)}, u32[]{:S(2)}, u32[]{:S(2)}) async-start(f32[128,2,16,128]{3,2,1,0:T(8,128)} %stack.49), calls=%async_computation.3 | async-start | bytes 4194304 | tf_op jit(solution)/shard_map/all_to_all | solution.py:133
  560.8 156.3 %all-reduce.11.cloned.1.call-start = ((), (), s32[]{:S(2)}) async-start(), calls=%async_computation.7 | async-start | bytes 524288 | tf_op jit(solution)/shard_map/psum | solution.py:139
  560.8 2.8 collective-permute-start.6
  562.3 4.6 collective-permute-start.7
  666.1 51.1 %copy-start.9 = (f32[1,512,128]{1,0,2:T(1,128)S(1)}, f32[1,512,128]{1,0,2:T(1,128)}, u32[]{:S(2)}) copy-start(f32[1,512,128]{1,0,2:T(1,128)} %copy.52) | copy-start | bytes 786436
  725.3 502.8 %copy-start.6 = (f32[512,128]{0,1:T(8,128)S(1)}, f32[512,128]{0,1:T(8,128)}, u32[]{:S(2)}) copy-start(f32[512,128]{0,1:T(8,128)} %all-reduce.9.cloned.1.call-done) | copy-start | bytes 786436
  725.3 502.8 %copy-start.7 = (f32[512,128]{0,1:T(8,128)S(1)}, f32[512,128]{0,1:T(8,128)}, u32[]{:S(2)}) copy-start(f32[512,128]{0,1:T(8,128)} %copy.41) | copy-start | bytes 786436
  725.3 502.8 %copy-start.8 = (f32[512,128]{0,1:T(8,128)S(1)}, f32[512,128]{0,1:T(8,128)}, u32[]{:S(2)}) copy-start(f32[512,128]{0,1:T(8,128)} %copy.42) | copy-start | bytes 786436
  (9 other events, 149.1 us)
Sparse Core Ops, SparseCore 0:
  134.4 52.3 all-reduce.4
  310.9 52.5 all-reduce.6
  487.7 52.5 all-reduce.8
  664.5 52.5 all-reduce.10
